TPU v7x, 512 devices: a whole 4x8x8 slice. The times are simulated.
512 devices in a mesh: chain: 2 (over core), sector: 256 (over z, y, x).
Axes of the slice: x: 4, y: 8, z: 8, core: 2. Of those that a mesh axis runs over, the one named last changes fastest.
Arguments:
- env_first: bfloat16 [2, 256, 15, 128, 128], P(None, 'sector'), may hold values from -6 to 6
- states: bfloat16 [2, 2, 4, 256, 128, 128], P('chain', None, None, 'sector'), may hold values from -0.5 to 0.5
- mpo: bfloat16 [2, 4, 15, 15], P('chain'), may hold values from -1.5 to 1.5
- block_rows: int32 [2, 256], P('chain', 'sector'), may hold values from 1 to 128, 16384 in all within a row
- present: int32 [2, 4, 256], P('chain', None, 'sector'), may hold values 0 or 1
Outputs:
- env_out: bfloat16 [2, 2, 256, 15, 128, 128], P('chain', None, 'sector')
Inputs may be any that keep to these rules, and one draw needn't show every extreme that they name: `block_rows`: in each site's row the 256 live sizes add up to 16384, and one of them equals 128.
All inputs are finite; a program needn't handle non-finite values. No bound on the sum of `block_rows` or of `present` on one device may be relied on, other than what follows from the above.
Results may differ from a plain program's by a relative error of at most 0.008.
Values may be sent and summed in bfloat16 or wider, within the bound.
A program may use at most 128 MiB of HBM per device.

v0:
```python
import jax
import jax.numpy as jnp
from jax import lax
from jax.sharding import PartitionSpec as P

QD = 4


def from_behind(value, axis, steps):
    count = lax.axis_size(axis)
    initial, last = (max(0, -steps), min(count, count - steps))
    return lax.ppermute(value, axis, [(source, source + steps) for source in range(initial, last)])


def state_mask(exists, inside_grid):
    state_ids = jnp.arange(exists.shape[0])
    return exists.astype(jnp.float32) * jnp.where(
        state_ids >= 2, inside_grid.astype(jnp.float32), 1.0
    )


def contract(incoming, blocks, coupling, exists, inside_grid):
    projected = jnp.einsum(
        "gwab,gsbc->gswac", incoming, blocks, preferred_element_type=jnp.float32
    ).astype(jnp.bfloat16)
    sandwich = jnp.einsum(
        "gsad,gswac->gswdc", blocks, projected, preferred_element_type=jnp.float32
    )
    coupled = jnp.einsum(
        "gswdc,swv->gsvdc", sandwich, coupling.astype(jnp.float32), precision=lax.Precision.HIGHEST
    )
    keep_mask = state_mask(exists, inside_grid)
    return (coupled * keep_mask[None, :, None, None, None]).astype(jnp.bfloat16)


def deliver(partials, rows_live):
    from_down = from_behind(partials[:, 2], "sector", 1)
    from_up = from_behind(partials[:, 1], "sector", QD)
    from_both = from_behind(partials[:, 3], "sector", QD + 1)
    summed = (
        partials[:, 0].astype(jnp.float32)
        + from_down.astype(jnp.float32)
        + from_up.astype(jnp.float32)
        + from_both.astype(jnp.float32)
    )
    block_width = partials.shape[-1]
    live_rows = jnp.arange(block_width) < rows_live
    live_mask = live_rows[:, None] & live_rows[None, :]
    return jnp.where(live_mask, summed, 0.0).astype(jnp.bfloat16)


def on_device(env_first, states, mpo, block_rows, present):
    chains = lax.axis_size("chain")
    chain_id = lax.axis_index("chain")
    down_charge = lax.axis_index("sector") % QD
    inside_grid = down_charge < QD - 1
    targets = env_first.shape[0]
    starting = env_first[:, 0]
    result = jnp.zeros_like(starting)
    blocks = states[0, :, :, 0]
    coupling = mpo[0]
    exists = present[0, :, 0]
    rows_live = block_rows[0, 0]
    current = starting
    zero_parts = jnp.zeros((targets, blocks.shape[1]) + starting.shape[1:], jnp.bfloat16)
    for step_number in range(chains):
        active = chain_id == step_number
        partials = lax.cond(
            active,
            lambda incoming: contract(incoming, blocks, coupling, exists, inside_grid),
            lambda incoming: zero_parts,
            current,
        )
        renewed = deliver(partials, rows_live)
        result = jnp.where(active, renewed, result)
        if step_number + 1 < chains:
            passed = from_behind(renewed, "chain", 1)
            current = jnp.where(chain_id == step_number + 1, passed, current)
    return result[None, :, None]


def solution(mesh):
    placed = (
        P(None, "sector", None, None, None),
        P("chain", None, None, "sector", None, None),
        P("chain", None, None, None),
        P("chain", "sector"),
        P("chain", None, "sector"),
    )
    return jax.shard_map(
        on_device,
        mesh=mesh,
        in_specs=placed,
        out_specs=P("chain", None, "sector", None, None, None),
        check_vma=False,
    )
```

profile of v0, /device:TPU:321, one launch (start us, length us, event | category | flops | bytes accessed | tf_op | source)
XLA Modules:
  0.0 204.4 jit_solution(345145049288147587)
XLA Ops:
  0.0 0.8 copy.6
  0.8 2.5 %conditional.2 = (bf16[2,4,15,128,128]{4,2,3,0,1:T(8,128)(2,1)}) conditional(s32[]{:T(128)} %convert_element_type.81, () %tuple.18, (bf16[2,4,128,128]{3,2,1,0:T(8,128)(2,1)}, bf16[2,15,128,128]{3,2,1,0:T(8,128)(2,1)}, bf16[4,15,15]{1,2,0:T(8,128)(2,1)S(1)}, s32[4]{0:T(128)}, pred[]{:T(512)}) %tuple.37), branch_computations={%region_0.1_spmd, %region_1.2_spmd} | conditional | flops 1364459520 | bytes 53675968 | solution.py:68
  0.8 2.5 %broadcast_in_dim.32 = bf16[2,4,15,128,128]{4,2,3,0,1:T(8,128)(2,1)} broadcast(bf16[]{:T(256)} %constant.10.clone), dimensions={} | broadcast | bytes 3932162 | tf_op jit(solution)/shard_map/broadcast_in_dim | solution.py:65
  3.4 2.9 %fusion.39 = (bf16[2,1,15,128,128]{4,2,3,0,1:T(8,128)(2,1)S(1)}, bf16[2,1,15,128,128]{4,2,3,0,1:T(8,128)(2,1)S(1)}, bf16[2,1,15,128,128]{4,2,3,0,1:T(8,128)(2,1)S(1)}, bf16[2,1,15,128,128]{4,2,3,0,1:T(8,128)(2,1)S(1)}) fusion(bf16[2,4,15,128,128]{4,2,3,0,1:T(8,128)(2,1)} %get-tuple-element.57), kind=kLoop, calls=%fused_computation.54 | loop fusion | bytes 7864320 | tf_op jit(solution)/shard_map/slice | solution.py:41
  6.3 0.3 copy.64
  6.6 3.1 %collective-permute-start = (bf16[2,15,128,128]{3,2,1,0:T(8,128)(2,1)S(1)}, bf16[2,15,128,128]{3,2,1,0:T(8,128)(2,1)S(1)}, u32[]{:S(2)}, u32[]{:S(2)}) collective-permute-start(bf16[2,15,128,128]{3,2,1,0:T(8,128)(2,1)S(1)} %bitcast.98), channel_id=1, source_target_pairs={{0,1},{1,2},{2,3},{3,4},{4,5},{5,6},{6,7},{7,8},{8,9},{9,10},{10,1... | collective-permute-start | bytes 2949128 | tf_op jit(solution)/shard_map/ppermute | solution.py:12
  9.7 0.0 copy-start
  9.7 0.0 copy-start.2
  9.7 0.0 copy-start.3
  9.7 0.3 copy.63
  10.0 3.3 %collective-permute-start.1 = (bf16[2,15,128,128]{3,2,1,0:T(8,128)(2,1)S(1)}, bf16[2,15,128,128]{3,2,1,0:T(8,128)(2,1)S(1)}, u32[]{:S(2)}, u32[]{:S(2)}) collective-permute-start(bf16[2,15,128,128]{3,2,1,0:T(8,128)(2,1)S(1)} %bitcast.99), channel_id=1, source_target_pairs={{0,4},{1,5},{2,6},{3,7},{4,8},{5,9},{6,10},{7,11},{8,12},{9,13},{1... | collective-permute-start | bytes 2949128 | tf_op jit(solution)/shard_map/ppermute | solution.py:12
  13.3 0.3 copy.62
  13.6 4.1 %collective-permute-start.2 = (bf16[2,15,128,128]{3,2,1,0:T(8,128)(2,1)S(1)}, bf16[2,15,128,128]{3,2,1,0:T(8,128)(2,1)S(1)}, u32[]{:S(2)}, u32[]{:S(2)}) collective-permute-start(bf16[2,15,128,128]{3,2,1,0:T(8,128)(2,1)S(1)} %bitcast.100), channel_id=1, source_target_pairs={{0,5},{1,6},{2,7},{3,8},{4,9},{5,10},{6,11},{7,12},{8,13},{9,14},{... | collective-permute-start | bytes 2949128 | tf_op jit(solution)/shard_map/ppermute | solution.py:12
  18.4 0.1 broadcast_and_fusion
  18.5 7.1 %collective-permute-done = bf16[2,15,128,128]{3,2,1,0:T(8,128)(2,1)S(1)} collective-permute-done((bf16[2,15,128,128]{3,2,1,0:T(8,128)(2,1)S(1)}, bf16[2,15,128,128]{3,2,1,0:T(8,128)(2,1)S(1)}, u32[]{:S(2)}, u32[]{:S(2)}) %collective-permute-start) | collective-permute-done | bytes 983072 | tf_op jit(solution)/shard_map/ppermute | solution.py:12
  25.6 1.5 collective-permute-done.1
  27.1 30.3 %collective-permute-done.2 = bf16[2,15,128,128]{3,2,1,0:T(8,128)(2,1)S(1)} collective-permute-done((bf16[2,15,128,128]{3,2,1,0:T(8,128)(2,1)S(1)}, bf16[2,15,128,128]{3,2,1,0:T(8,128)(2,1)S(1)}, u32[]{:S(2)}, u32[]{:S(2)}) %collective-permute-start.2) | collective-permute-done | bytes 983072 | tf_op jit(solution)/shard_map/ppermute | solution.py:12
  57.4 0.6 fusion.35
  58.1 1.3 collective-permute-start.3
  59.4 37.2 %collective-permute-done.3 = bf16[2,15,128,128]{3,2,1,0:T(8,128)(2,1)S(1)} collective-permute-done((bf16[2,15,128,128]{3,2,1,0:T(8,128)(2,1)S(1)}, bf16[2,15,128,128]{3,2,1,0:T(8,128)(2,1)S(1)}, u32[]{:S(2)}, u32[]{:S(2)}) %collective-permute-start.3) | collective-permute-done | bytes 983072 | tf_op jit(solution)/shard_map/ppermute | solution.py:12
  96.6 0.0 copy-done
  96.6 0.0 copy-done.2
  96.6 0.0 copy-done.3
  96.6 29.3 %conditional.3 = (bf16[2,4,15,128,128]{4,2,3,0,1:T(8,128)(2,1)}) conditional(s32[]{:T(128)} %convert_element_type.80, () %tuple.17, (pred[]{:T(512)}, bf16[2,15,128,128]{3,2,1,0:T(8,128)(2,1)S(1)}, bf16[2,15,128,128]{3,2,1,0:T(8,128)(2,1)S(1)}, bf16[2,4,128,128]{3,2,1,0:T(8,128)(2,1)S(1)}, bf16[4,15,15]{1,2,0:T(8,128)(2,1)S(1)}, ...), branch_computations={%region_2.3_spmd, %region_3.4_spmd} | conditional | flops 1366917120 | bytes 53610312 | solution.py:68
  96.6 1.2 convolution_convert_fusion
  97.8 3.7 %copy.58 = bf16[2,15,128,4,128]{4,3,2,1,0:T(4,128)(2,1)S(1)} copy(bf16[2,15,128,4,128]{4,2,3,1,0:T(8,128)(2,1)S(1)} %convolution_convert_fusion) | data formatting | bytes 7864320 | tf_op jit(solution)/shard_map/cond
  101.5 4.4 %fusion.17 = f32[2,4,15,128,128]{4,3,2,1,0:T(8,128)} fusion(bf16[2,4,15,128,128]{4,1,3,2,0:T(4,128)(2,1)S(1)} %bitcast.93, bf16[2,4,128,128]{3,2,1,0:T(8,128)(2,1)S(1)} %get-tuple-element.45), kind=kOutput, calls=%fused_computation.20 | convolution fusion | flops 503316480 | bytes 12058624 | tf_op jit(solution)/shard_map/cond/branch_1_fun/gsad,gswac->gswdc/dot_general | solution.py:26
  105.9 10.1 %copy.26 = f32[2,4,15,128,128]{3,2,4,0,1:T(8,128)} copy(f32[2,4,15,128,128]{4,3,2,1,0:T(8,128)} %fusion.17) | data formatting | bytes 15728640 | tf_op jit(solution)/shard_map/cond/branch_1_fun/gsad,gswac->gswdc/dot_general | solution.py:26
  116.0 10.0 %fusion.16 = bf16[2,4,15,128,128]{4,2,3,0,1:T(8,128)(2,1)} fusion(f32[4]{0:T(128)S(1)} %fusion.27, f32[2,4,15,128,128]{3,2,4,0,1:T(8,128)} %copy.26, bf16[4,15,15]{1,2,0:T(8,128)(2,1)S(1)} %get-tuple-element.46), kind=kOutput, calls=%fused_computation.18 | convolution fusion | flops 357826560 | bytes 11798296 | tf_op jit(solution)/shard_map/cond/branch_1_fun/gswdc,swv->gsvdc/dot_general | solution.py:29
  126.0 2.9 %fusion.38 = (bf16[2,1,15,128,128]{4,2,3,0,1:T(8,128)(2,1)S(1)}, bf16[2,1,15,128,128]{4,2,3,0,1:T(8,128)(2,1)S(1)}, bf16[2,1,15,128,128]{4,2,3,0,1:T(8,128)(2,1)S(1)}, bf16[2,1,15,128,128]{4,2,3,0,1:T(8,128)(2,1)S(1)}) fusion(bf16[2,4,15,128,128]{4,2,3,0,1:T(8,128)(2,1)} %get-tuple-element.58), kind=kLoop, calls=%fused_computation.53 | loop fusion | bytes 7864320 | tf_op jit(solution)/shard_map/slice | solution.py:41
  128.9 0.3 copy.61
  129.2 1.9 collective-permute-start.4
  131.1 0.3 copy.60
  131.4 10.5 %collective-permute-start.5 = (bf16[2,15,128,128]{3,2,1,0:T(8,128)(2,1)S(1)}, bf16[2,15,128,128]{3,2,1,0:T(8,128)(2,1)S(1)}, u32[]{:S(2)}, u32[]{:S(2)}) collective-permute-start(bf16[2,15,128,128]{3,2,1,0:T(8,128)(2,1)S(1)} %bitcast.102), channel_id=1, source_target_pairs={{0,4},{1,5},{2,6},{3,7},{4,8},{5,9},{6,10},{7,11},{8,12},{9,13},{1... | collective-permute-start | bytes 2949128 | tf_op jit(solution)/shard_map/ppermute | solution.py:12
  141.9 0.3 copy.59
  142.2 1.9 collective-permute-start.6
  144.1 12.7 %collective-permute-done.4 = bf16[2,15,128,128]{3,2,1,0:T(8,128)(2,1)S(1)} collective-permute-done((bf16[2,15,128,128]{3,2,1,0:T(8,128)(2,1)S(1)}, bf16[2,15,128,128]{3,2,1,0:T(8,128)(2,1)S(1)}, u32[]{:S(2)}, u32[]{:S(2)}) %collective-permute-start.4) | collective-permute-done | bytes 983072 | tf_op jit(solution)/shard_map/ppermute | solution.py:12
  156.8 0.0 collective-permute-done.5
  156.8 45.8 %collective-permute-done.6 = bf16[2,15,128,128]{3,2,1,0:T(8,128)(2,1)S(1)} collective-permute-done((bf16[2,15,128,128]{3,2,1,0:T(8,128)(2,1)S(1)}, bf16[2,15,128,128]{3,2,1,0:T(8,128)(2,1)S(1)}, u32[]{:S(2)}, u32[]{:S(2)}) %collective-permute-start.6) | collective-permute-done | bytes 983072 | tf_op jit(solution)/shard_map/ppermute | solution.py:12
  202.6 1.8 fusion.37
  (2 shorter events, 0.0 us)
Async XLA Ops:
  6.6 19.1 %collective-permute-start = (bf16[2,15,128,128]{3,2,1,0:T(8,128)(2,1)S(1)}, bf16[2,15,128,128]{3,2,1,0:T(8,128)(2,1)S(1)}, u32[]{:S(2)}, u32[]{:S(2)}) collective-permute-start(bf16[2,15,128,128]{3,2,1,0:T(8,128)(2,1)S(1)} %bitcast.98), channel_id=1, source_target_pairs={{0,1},{1,2},{2,3},{3,4},{4,5},{5,6},{6,7},{7,8},{8,9},{9,10},{10,1... | collective-permute-start | bytes 2949128 | tf_op jit(solution)/shard_map/ppermute | solution.py:12
  9.7 86.9 %copy-start = (bf16[1,2,4,1,128,128]{5,4,3,2,1,0:T(8,128)(2,1)S(1)}, bf16[1,2,4,1,128,128]{5,4,3,2,1,0:T(8,128)(2,1)}, u32[]{:S(2)}) copy-start(bf16[1,2,4,1,128,128]{5,4,3,2,1,0:T(8,128)(2,1)} %param.10) | copy-start | bytes 786436
  9.7 86.9 %copy-start.2 = (bf16[2,1,15,128,128]{4,3,2,1,0:T(8,128)(2,1)S(1)}, bf16[2,1,15,128,128]{4,3,2,1,0:T(8,128)(2,1)}, u32[]{:S(2)}) copy-start(bf16[2,1,15,128,128]{4,3,2,1,0:T(8,128)(2,1)} %param.9) | copy-start | bytes 2949124
  9.7 86.9 %copy-start.3 = (s32[1,4,1]{1,2,0:T(1,128)S(1)}, s32[1,4,1]{1,2,0:T(1,128)}, u32[]{:S(2)}) copy-start(s32[1,4,1]{1,2,0:T(1,128)} %param.13) | copy-start | bytes 52
  10.0 17.1 %collective-permute-start.1 = (bf16[2,15,128,128]{3,2,1,0:T(8,128)(2,1)S(1)}, bf16[2,15,128,128]{3,2,1,0:T(8,128)(2,1)S(1)}, u32[]{:S(2)}, u32[]{:S(2)}) collective-permute-start(bf16[2,15,128,128]{3,2,1,0:T(8,128)(2,1)S(1)} %bitcast.99), channel_id=1, source_target_pairs={{0,4},{1,5},{2,6},{3,7},{4,8},{5,9},{6,10},{7,11},{8,12},{9,13},{1... | collective-permute-start | bytes 2949128 | tf_op jit(solution)/shard_map/ppermute | solution.py:12
  13.6 43.8 %collective-permute-start.2 = (bf16[2,15,128,128]{3,2,1,0:T(8,128)(2,1)S(1)}, bf16[2,15,128,128]{3,2,1,0:T(8,128)(2,1)S(1)}, u32[]{:S(2)}, u32[]{:S(2)}) collective-permute-start(bf16[2,15,128,128]{3,2,1,0:T(8,128)(2,1)S(1)} %bitcast.100), channel_id=1, source_target_pairs={{0,5},{1,6},{2,7},{3,8},{4,9},{5,10},{6,11},{7,12},{8,13},{9,14},{... | collective-permute-start | bytes 2949128 | tf_op jit(solution)/shard_map/ppermute | solution.py:12
  58.1 38.5 %collective-permute-start.3 = (bf16[2,15,128,128]{3,2,1,0:T(8,128)(2,1)S(1)}, bf16[2,15,128,128]{3,2,1,0:T(8,128)(2,1)S(1)}, u32[]{:S(2)}, u32[]{:S(2)}) collective-permute-start(bf16[2,15,128,128]{3,2,1,0:T(8,128)(2,1)S(1)} %fusion.35), channel_id=1, source_target_pairs={{0,256},{1,257},{2,258},{3,259},{4,260},{5,261},{6,262},{7,263},{8... | collective-permute-start | bytes 2949128 | tf_op jit(solution)/shard_map/ppermute | solution.py:12
  129.2 27.6 %collective-permute-start.4 = (bf16[2,15,128,128]{3,2,1,0:T(8,128)(2,1)S(1)}, bf16[2,15,128,128]{3,2,1,0:T(8,128)(2,1)S(1)}, u32[]{:S(2)}, u32[]{:S(2)}) collective-permute-start(bf16[2,15,128,128]{3,2,1,0:T(8,128)(2,1)S(1)} %bitcast.101), channel_id=1, source_target_pairs={{0,1},{1,2},{2,3},{3,4},{4,5},{5,6},{6,7},{7,8},{8,9},{9,10},{10,1... | collective-permute-start | bytes 2949128 | tf_op jit(solution)/shard_map/ppermute | solution.py:12
  131.4 25.4 %collective-permute-start.5 = (bf16[2,15,128,128]{3,2,1,0:T(8,128)(2,1)S(1)}, bf16[2,15,128,128]{3,2,1,0:T(8,128)(2,1)S(1)}, u32[]{:S(2)}, u32[]{:S(2)}) collective-permute-start(bf16[2,15,128,128]{3,2,1,0:T(8,128)(2,1)S(1)} %bitcast.102), channel_id=1, source_target_pairs={{0,4},{1,5},{2,6},{3,7},{4,8},{5,9},{6,10},{7,11},{8,12},{9,13},{1... | collective-permute-start | bytes 2949128 | tf_op jit(solution)/shard_map/ppermute | solution.py:12
  142.2 60.5 %collective-permute-start.6 = (bf16[2,15,128,128]{3,2,1,0:T(8,128)(2,1)S(1)}, bf16[2,15,128,128]{3,2,1,0:T(8,128)(2,1)S(1)}, u32[]{:S(2)}, u32[]{:S(2)}) collective-permute-start(bf16[2,15,128,128]{3,2,1,0:T(8,128)(2,1)S(1)} %bitcast.103), channel_id=1, source_target_pairs={{0,5},{1,6},{2,7},{3,8},{4,9},{5,10},{6,11},{7,12},{8,13},{9,14},{... | collective-permute-start | bytes 2949128 | tf_op jit(solution)/shard_map/ppermute | solution.py:12
where the time goes:
time: 205 us; the launch traced here: 204 us
  waiting for transfers between devices  135 us (66%)
  starting transfers between devices  26.2 us (13%)
  local copies, waits for them, and re-layouts  24.5 us (12%)
  matrix products  15.6 us (8%)
  other arithmetic  2.56 us (1%)
    ppermute x7, waiting for transfers between devices, from_behind(): lax.ppermute(value, axis, [(source, source + steps) for source in range(i...  135 us
    ppermute x7, starting transfers between devices, from_behind(): lax.ppermute(value, axis, [(source, source + steps) for source in range(i...  26.2 us
    dot_general x1, local copies, waits for them, and re-layouts, contract(): jnp.einsum('gsad,gswac->gswdc', blocks, projected, preferred_element_type...  10.1 us
    dot_general x1, matrix products, contract(): jnp.einsum('gswdc,swv->gsvdc', sandwich, coupling.astype(jnp.float32), pr...  9.98 us
    slice x2, local copies, waits for them, and re-layouts, deliver(): partials[:, 0].astype(jnp.float32) + from_down.astype(jnp.float32)  5.86 us
    dot_general x1, matrix products, contract(): jnp.einsum('gsad,gswac->gswdc', blocks, projected, preferred_element_type...  4.4 us
  transfers between devices with their start and end apart: 7, of which 6 were waited for; matrix products, arithmetic and copies ran while one was open for 1% of the time, Pallas kernels for 0%

commit v1 on v0

v1 whole, which is shorter than its diff:
```python
import jax
import jax.numpy as jnp
from jax import lax
from jax.experimental import pallas as pl
from jax.experimental.pallas import tpu as pltpu
from jax.sharding import PartitionSpec as P

QD = 4
W = 15
BLK = 128
SUB = 16
CHUNK = 5
CHUNKS = W // CHUNK
MESH = pl.DeviceIdType.MESH
BF = jnp.bfloat16
F32 = jnp.float32


def kernel(
    env_in, states_in, pack_in, out,
    env, blocks, pack, joined, turned, kron, proj, mixed, parts, got,
    env_sem, own_sem, part_send, part_recv, swap_send, swap_recv, out_sem, out_send, out_recv,
):
    sectors = lax.axis_size("sector")
    core, k = lax.axis_index("chain"), lax.axis_index("sector")
    other = 1 - core
    down = lax.rem(k, QD)
    goes_right, comes_left = down < QD - 1, down > 0
    goes_up, comes_below = k < sectors - QD, k >= QD
    routes = {
        1: (QD, goes_up, comes_below),
        2: (1, goes_right, comes_left),
        3: (QD + 1, goes_right & goes_up, comes_left & comes_below),
    }

    env_copies = [
        pltpu.make_async_copy(
            env_in.at[core, 0, pl.ds(c * CHUNK, CHUNK)], env.at[0, pl.ds(c * CHUNK, CHUNK)], env_sem.at[c]
        )
        for c in range(CHUNKS)
    ]
    own_blocks = pltpu.make_async_copy(states_in.at[0, core, :, 0], blocks.at[core], own_sem.at[0])
    own_pack = pltpu.make_async_copy(pack_in, pack.at[core], own_sem.at[1])
    own_blocks.start()
    own_pack.start()
    for copy in env_copies:
        copy.start()

    barrier = pltpu.get_barrier_semaphore()
    pl.semaphore_signal(barrier, inc=1, device_id=(other, k), device_id_type=MESH)
    for step, sends, receives in routes.values():
        @pl.when(sends)
        def _():
            pl.semaphore_signal(barrier, inc=1, device_id=(core, k + step), device_id_type=MESH)

        @pl.when(receives)
        def _():
            pl.semaphore_signal(barrier, inc=1, device_id=(core, k - step), device_id_type=MESH)

    peers = 1
    for step, sends, receives in routes.values():
        peers = peers + sends.astype(jnp.int32) + receives.astype(jnp.int32)
    pl.semaphore_wait(barrier, peers)

    swaps = [
        pltpu.make_async_remote_copy(
            src_ref=source, dst_ref=target, send_sem=swap_send.at[i], recv_sem=swap_recv.at[i],
            device_id=(other, k), device_id_type=MESH,
        )
        for i, (source, target) in enumerate(
            [(pack_in, pack.at[core]), (states_in.at[0, other, :, 0], blocks.at[core])]
        )
    ]
    for swap in swaps:
        swap.start()

    proj[W] = jnp.zeros((BLK, 4 * BLK), BF)
    for s, (step, sends, receives) in routes.items():
        @pl.when(jnp.logical_not(receives))
        def _():
            for site in range(2):
                got[site, s - 1] = jnp.zeros((W, BLK, BLK), BF)

    def await_site(site):
        @pl.when(core == site)
        def _():
            own_blocks.wait()
            own_pack.wait()

        @pl.when(core != site)
        def _():
            for swap in swaps:
                swap.wait_recv()

    def prepare(site):
        spread = (lax.broadcasted_iota(jnp.int32, (W * SUB, SUB), 0) >> 4) == lax.broadcasted_iota(
            jnp.int32, (W * SUB, SUB), 1
        )
        spread = jnp.where(spread, 1.0, 0.0).astype(BF)
        widen = lax.broadcasted_iota(jnp.int32, (BLK, 256), 0) == (
            lax.broadcasted_iota(jnp.int32, (BLK, 256), 1) >> 4
        )
        widen = jnp.where(widen, 1.0, 0.0).astype(BF)
        same = (lax.broadcasted_iota(jnp.int32, (W * SUB, 256), 0) & 15) == (
            lax.broadcasted_iota(jnp.int32, (W * SUB, 256), 1) & 15
        )
        for s in range(4):
            tall = jnp.dot(spread, pack[site, s], preferred_element_type=F32).astype(BF)
            wide = jnp.dot(tall, widen, preferred_element_type=F32)
            kron[s] = jnp.where(same, wide, 0.0).astype(BF)
            block = blocks[site, s]
            joined[:, s * BLK:(s + 1) * BLK] = block
            turned[s] = block.astype(F32).T.astype(BF)

    def project(site, c):
        rows = env[site, c * CHUNK:(c + 1) * CHUNK].reshape(CHUNK * BLK, BLK)
        product = jnp.dot(rows, joined[...], preferred_element_type=F32).astype(BF)
        proj[c * CHUNK:(c + 1) * CHUNK] = product.reshape(CHUNK, BLK, 4 * BLK)

    def part_copy(site, s, c):
        step = routes[s][0]
        span = pl.ds(c * CHUNK, CHUNK)
        return pltpu.make_async_remote_copy(
            src_ref=parts.at[site, s, span], dst_ref=got.at[site, s - 1, span],
            send_sem=part_send.at[site, s - 1, c], recv_sem=part_recv.at[site, s - 1, c],
            device_id=(core, k + step), device_id_type=MESH,
        )

    def mix_and_send(site, s):
        lanes = slice(s * BLK, (s + 1) * BLK)
        for i in range(BLK // (2 * SUB)):
            low, mid, high = 2 * i * SUB, (2 * i + 1) * SUB, (2 * i + 2) * SUB
            right = jnp.concatenate(
                [proj[:, low:mid, lanes].reshape(256, BLK), proj[:, mid:high, lanes].reshape(256, BLK)], axis=1
            )
            product = jnp.dot(kron[s], right, preferred_element_type=F32).astype(BF)
            for v in range(W):
                mixed[low:mid, v * BLK:(v + 1) * BLK] = product[v * SUB:(v + 1) * SUB, :BLK]
                mixed[mid:high, v * BLK:(v + 1) * BLK] = product[v * SUB:(v + 1) * SUB, BLK:]
        for c in range(CHUNKS):
            product = jnp.dot(
                turned[s], mixed[:, c * CHUNK * BLK:(c + 1) * CHUNK * BLK], preferred_element_type=F32
            ).astype(BF)
            for v in range(CHUNK):
                parts[site, s, c * CHUNK + v] = product[:, v * BLK:(v + 1) * BLK]
            if s:
                @pl.when(routes[s][1])
                def _():
                    part_copy(site, s, c).start()

    def out_copies(site, c):
        span = pl.ds(c * CHUNK, CHUNK)
        source, target = env.at[site + 1, span], out.at[0, core, 0, span]
        local = pltpu.make_async_copy(source, target, out_sem.at[c])
        remote = pltpu.make_async_remote_copy(
            src_ref=source, dst_ref=target, send_sem=out_send.at[c], recv_sem=out_recv.at[c],
            device_id=(other, k), device_id_type=MESH,
        )
        return local, remote

    def combine(site, c):
        for s, (step, sends, receives) in routes.items():
            @pl.when(receives)
            def _():
                part_copy(site, s, c).wait_recv()

        size = pack[site, 4].astype(F32)[0:1]
        live = (lax.broadcasted_iota(jnp.int32, (BLK, BLK), 0).astype(F32) < size) & (
            lax.broadcasted_iota(jnp.int32, (BLK, BLK), 1).astype(F32) < size
        )
        for v in range(c * CHUNK, (c + 1) * CHUNK):
            total = parts[site, 0, v].astype(F32) + got[site, 1, v].astype(F32)
            total = total + got[site, 0, v].astype(F32) + got[site, 2, v].astype(F32)
            env[site + 1, v] = jnp.where(live, total, 0.0).astype(BF)
        local, remote = out_copies(site, c)

        @pl.when(core == site)
        def _():
            local.start()

        @pl.when(core != site)
        def _():
            remote.start()

    for site in range(2):
        await_site(site)
        prepare(site)
        for c in range(CHUNKS):
            if site == 0:
                env_copies[c].wait()
            else:
                combine(0, c)
            project(site, c)
        for s in (3, 2, 1, 0):
            mix_and_send(site, s)
    for c in range(CHUNKS):
        combine(1, c)

    for swap in swaps:
        swap.wait_send()
    for site in range(2):
        for s, (step, sends, receives) in routes.items():
            @pl.when(sends)
            def _():
                for c in range(CHUNKS):
                    part_copy(site, s, c).wait_send()
    for site in range(2):
        for c in range(CHUNKS):
            local, remote = out_copies(site, c)

            @pl.when(core == site)
            def _():
                local.wait()
                remote.wait_recv()

            @pl.when(core != site)
            def _():
                remote.wait_send()


def on_device(env_first, states, mpo, block_rows, present):
    down_charge = lax.axis_index("sector") % QD
    inside = jnp.where(jnp.arange(4) >= 2, (down_charge < QD - 1).astype(F32), 1.0)
    keep = present[0, :, 0].astype(F32) * inside
    coupling = jnp.swapaxes(mpo[0], 1, 2).astype(F32) * keep[:, None, None]
    coupling = jnp.pad(coupling, ((0, 0), (0, SUB - W), (0, BLK - W)))
    size = jnp.broadcast_to(block_rows[0, 0].astype(F32), (1, SUB, BLK))
    pack = jnp.concatenate([coupling, size], axis=0).astype(BF)
    anywhere = pl.BlockSpec(memory_space=pl.ANY)
    return pl.pallas_call(
        kernel,
        out_shape=jax.ShapeDtypeStruct((1, 2, 1, W, BLK, BLK), BF),
        in_specs=[anywhere] * 3,
        out_specs=anywhere,
        scratch_shapes=[
            pltpu.VMEM((3, W, BLK, BLK), BF),
            pltpu.VMEM((2, 4, BLK, BLK), BF),
            pltpu.VMEM((2, 5, SUB, BLK), BF),
            pltpu.VMEM((BLK, 4 * BLK), BF),
            pltpu.VMEM((4, BLK, BLK), BF),
            pltpu.VMEM((4, W * SUB, 256), BF),
            pltpu.VMEM((W + 1, BLK, 4 * BLK), BF),
            pltpu.VMEM((BLK, W * BLK), BF),
            pltpu.VMEM((2, 4, W, BLK, BLK), BF),
            pltpu.VMEM((2, 3, W, BLK, BLK), BF),
            pltpu.SemaphoreType.DMA((CHUNKS,)),
            pltpu.SemaphoreType.DMA((2,)),
            pltpu.SemaphoreType.DMA((2, 3, CHUNKS)),
            pltpu.SemaphoreType.DMA((2, 3, CHUNKS)),
            pltpu.SemaphoreType.DMA((2,)),
            pltpu.SemaphoreType.DMA((2,)),
            pltpu.SemaphoreType.DMA((CHUNKS,)),
            pltpu.SemaphoreType.DMA((CHUNKS,)),
            pltpu.SemaphoreType.DMA((CHUNKS,)),
        ],
        compiler_params=pltpu.CompilerParams(
            collective_id=0, has_side_effects=True, vmem_limit_bytes=48 * 1024 * 1024
        ),
    )(env_first, states, pack)


def solution(mesh):
    placed = (
        P(None, "sector", None, None, None),
        P("chain", None, None, "sector", None, None),
        P("chain", None, None, None),
        P("chain", "sector"),
        P("chain", None, "sector"),
    )
    return jax.shard_map(
        on_device,
        mesh=mesh,
        in_specs=placed,
        out_specs=P("chain", None, "sector", None, None, None),
        check_vma=False,
    )
```

time: 205 us -> 63.6 us (0.31)
  the two profiles are of different devices: /device:TPU:321 before, /device:TPU:19 now
where the time goes in v1:
time: 63.6 us; the launch traced here: 63.3 us
  Pallas kernels  58.7 us (92%)
  local copies, waits for them, and re-layouts  3.86 us (6%)
  between operations  0.7 us (1%)
    pallas_call x1, Pallas kernels, on_device(): pl.pallas_call(kernel, out_shape=jax.ShapeDtypeStruct((1, 2, 1, W, BLK, B...  58.7 us
    unnamed x10, local copies, waits for them, and re-layouts  3.86 us

profile of v1, /device:TPU:19, one launch (start us, length us, event | category | flops | bytes accessed | tf_op | source)
XLA Modules:
  0.0 63.3 jit_solution(16751140816421144580)
XLA Ops:
  0.0 0.0 copy-start.2
  0.7 0.0 copy-start.3
  0.7 0.6 %copy-done.3 = s32[1,4,1]{1,2,0:T(1,128)S(1)} copy-done((s32[1,4,1]{1,2,0:T(1,128)S(1)}, s32[1,4,1]{1,2,0:T(1,128)}, u32[]{:S(2)}) %copy-start.3) | copy-done | bytes 40
  1.3 0.0 copy-done.2
  1.3 0.1 copy.6
  1.4 0.1 fusion.2
  1.5 0.0 copy-start
  1.6 1.2 %copy-done = bf16[2,1,15,128,128]{4,3,2,1,0:T(8,128)(2,1)S(1)} copy-done((bf16[2,1,15,128,128]{4,3,2,1,0:T(8,128)(2,1)S(1)}, bf16[2,1,15,128,128]{4,3,2,1,0:T(8,128)(2,1)}, u32[]{:S(2)}) %copy-start) | copy-done | bytes 983064
  2.8 0.0 copy-start.1
  2.8 0.9 %copy-done.1 = bf16[1,2,4,1,128,128]{5,4,3,2,1,0:T(8,128)(2,1)S(1)} copy-done((bf16[1,2,4,1,128,128]{5,4,3,2,1,0:T(8,128)(2,1)S(1)}, bf16[1,2,4,1,128,128]{5,4,3,2,1,0:T(8,128)(2,1)}, u32[]{:S(2)}) %copy-start.1) | copy-done | bytes 262168
  3.7 58.7 %shard_map.55 = bf16[1,2,1,15,128,128]{5,4,3,2,1,0:T(8,128)(2,1)S(1)} custom-call(bf16[2,1,15,128,128]{4,3,2,1,0:T(8,128)(2,1)S(1)} %copy-done, bf16[1,2,4,1,128,128]{5,4,3,2,1,0:T(8,128)(2,1)S(1)} %copy-done.1, bf16[5,16,128]{2,1,0:T(8,128)(2,1)S(1)} %fusion.pack_in), custom_call_target="tpu_custom_call" | custom-call | tf_op jit(solution)/shard_map/pallas_call | solution.py:230
  62.4 0.9 %copy.9 = bf16[1,2,1,15,128,128]{5,4,3,2,1,0:T(8,128)(2,1)} copy(bf16[1,2,1,15,128,128]{5,4,3,2,1,0:T(8,128)(2,1)S(1)} %shard_map.55) | data formatting | bytes 1966080
  (2 shorter events, 0.0 us)
Async XLA Ops:
  0.0 1.3 %copy-start.2 = (bf16[1,4,15,15]{3,1,2,0:T(4,128)(2,1)S(1)}, bf16[1,4,15,15]{3,1,2,0:T(4,128)(2,1)}, u32[]{:S(2)}) copy-start(bf16[1,4,15,15]{3,1,2,0:T(4,128)(2,1)} %param.7) | copy-start | bytes 5404
  0.7 0.7 %copy-start.3 = (s32[1,4,1]{1,2,0:T(1,128)S(1)}, s32[1,4,1]{1,2,0:T(1,128)}, u32[]{:S(2)}) copy-start(s32[1,4,1]{1,2,0:T(1,128)} %param.9) | copy-start | bytes 52
  1.5 1.2 %copy-start = (bf16[2,1,15,128,128]{4,3,2,1,0:T(8,128)(2,1)S(1)}, bf16[2,1,15,128,128]{4,3,2,1,0:T(8,128)(2,1)}, u32[]{:S(2)}) copy-start(bf16[2,1,15,128,128]{4,3,2,1,0:T(8,128)(2,1)} %env_in.1) | copy-start | bytes 2949124
  2.8 0.9 %copy-start.1 = (bf16[1,2,4,1,128,128]{5,4,3,2,1,0:T(8,128)(2,1)S(1)}, bf16[1,2,4,1,128,128]{5,4,3,2,1,0:T(8,128)(2,1)}, u32[]{:S(2)}) copy-start(bf16[1,2,4,1,128,128]{5,4,3,2,1,0:T(8,128)(2,1)} %states_in.1) | copy-start | bytes 786436

commit v2 on v1

--- a/solution.py
+++ b/solution.py
@@ -9,8 +9,9 @@
 W = 15
 BLK = 128
 SUB = 16
-CHUNK = 5
-CHUNKS = W // CHUNK
+SPANS = ((0, 4), (4, 4), (8, 4), (12, 3))
+CHUNKS = len(SPANS)
+RIGHT_FIRST = (0, 1)
 MESH = pl.DeviceIdType.MESH
 BF = jnp.bfloat16
 F32 = jnp.float32
@@ -27,15 +28,20 @@
     down = lax.rem(k, QD)
     goes_right, comes_left = down < QD - 1, down > 0
     goes_up, comes_below = k < sectors - QD, k >= QD
-    routes = {
-        1: (QD, goes_up, comes_below),
-        2: (1, goes_right, comes_left),
-        3: (QD + 1, goes_right & goes_up, comes_left & comes_below),
-    }
+    peers_at = ((QD, goes_up, comes_below), (1, goes_right, comes_left))
+
+    def route(slot, c):
+        if slot == 0:
+            return 1, QD, goes_up, comes_below
+        if slot == 1:
+            return 2, 1, goes_right, comes_left
+        if c in RIGHT_FIRST:
+            return 3, 1, goes_right & goes_up, comes_left & goes_up
+        return 3, QD, goes_right & goes_up, comes_below & goes_right
 
     env_copies = [
         pltpu.make_async_copy(
-            env_in.at[core, 0, pl.ds(c * CHUNK, CHUNK)], env.at[0, pl.ds(c * CHUNK, CHUNK)], env_sem.at[c]
+            env_in.at[core, 0, pl.ds(*SPANS[c])], env.at[0, pl.ds(*SPANS[c])], env_sem.at[c]
         )
         for c in range(CHUNKS)
     ]
@@ -48,7 +54,7 @@
 
     barrier = pltpu.get_barrier_semaphore()
     pl.semaphore_signal(barrier, inc=1, device_id=(other, k), device_id_type=MESH)
-    for step, sends, receives in routes.values():
+    for step, sends, receives in peers_at:
         @pl.when(sends)
         def _():
             pl.semaphore_signal(barrier, inc=1, device_id=(core, k + step), device_id_type=MESH)
@@ -58,7 +64,7 @@
             pl.semaphore_signal(barrier, inc=1, device_id=(core, k - step), device_id_type=MESH)
 
     peers = 1
-    for step, sends, receives in routes.values():
+    for step, sends, receives in peers_at:
         peers = peers + sends.astype(jnp.int32) + receives.astype(jnp.int32)
     pl.semaphore_wait(barrier, peers)
 
@@ -75,11 +81,12 @@
         swap.start()
 
     proj[W] = jnp.zeros((BLK, 4 * BLK), BF)
-    for s, (step, sends, receives) in routes.items():
-        @pl.when(jnp.logical_not(receives))
-        def _():
-            for site in range(2):
-                got[site, s - 1] = jnp.zeros((W, BLK, BLK), BF)
+    for slot in range(3):
+        for c, (low, many) in enumerate(SPANS):
+            @pl.when(jnp.logical_not(route(slot, c)[3]))
+            def _():
+                for site in range(2):
+                    got[site, slot, low:low + many] = jnp.zeros((many, BLK, BLK), BF)
 
     def await_site(site):
         @pl.when(core == site)
@@ -113,18 +120,38 @@
             turned[s] = block.astype(F32).T.astype(BF)
 
     def project(site, c):
-        rows = env[site, c * CHUNK:(c + 1) * CHUNK].reshape(CHUNK * BLK, BLK)
+        low, many = SPANS[c]
+        rows = env[site, low:low + many].reshape(many * BLK, BLK)
         product = jnp.dot(rows, joined[...], preferred_element_type=F32).astype(BF)
-        proj[c * CHUNK:(c + 1) * CHUNK] = product.reshape(CHUNK, BLK, 4 * BLK)
-
-    def part_copy(site, s, c):
-        step = routes[s][0]
-        span = pl.ds(c * CHUNK, CHUNK)
+        proj[low:low + many] = product.reshape(many, BLK, 4 * BLK)
+
+    def part_copy(site, slot, c):
+        state, step = route(slot, c)[:2]
+        span = pl.ds(*SPANS[c])
         return pltpu.make_async_remote_copy(
-            src_ref=parts.at[site, s, span], dst_ref=got.at[site, s - 1, span],
-            send_sem=part_send.at[site, s - 1, c], recv_sem=part_recv.at[site, s - 1, c],
+            src_ref=parts.at[site, state, span], dst_ref=got.at[site, slot, span],
+            send_sem=part_send.at[site, slot, c], recv_sem=part_recv.at[site, slot, c],
             device_id=(core, k + step), device_id_type=MESH,
         )
+
+    def send(site, slot, c):
+        @pl.when(route(slot, c)[2])
+        def _():
+            part_copy(site, slot, c).start()
+
+    def receive(site, slot, c):
+        @pl.when(route(slot, c)[3])
+        def _():
+            part_copy(site, slot, c).wait_recv()
+
+    def pass_on(site, c):
+        slot = 0 if c in RIGHT_FIRST else 1
+        low, many = SPANS[c]
+        receive(site, 2, c)
+        for v in range(low, low + many):
+            both = parts[site, slot + 1, v].astype(F32) + got[site, 2, v].astype(F32)
+            parts[site, slot + 1, v] = both.astype(BF)
+        send(site, slot, c)
 
     def mix_and_send(site, s):
         lanes = slice(s * BLK, (s + 1) * BLK)
@@ -137,19 +164,21 @@
             for v in range(W):
                 mixed[low:mid, v * BLK:(v + 1) * BLK] = product[v * SUB:(v + 1) * SUB, :BLK]
                 mixed[mid:high, v * BLK:(v + 1) * BLK] = product[v * SUB:(v + 1) * SUB, BLK:]
-        for c in range(CHUNKS):
+        for c, (low, many) in enumerate(SPANS):
             product = jnp.dot(
-                turned[s], mixed[:, c * CHUNK * BLK:(c + 1) * CHUNK * BLK], preferred_element_type=F32
+                turned[s], mixed[:, low * BLK:(low + many) * BLK], preferred_element_type=F32
             ).astype(BF)
-            for v in range(CHUNK):
-                parts[site, s, c * CHUNK + v] = product[:, v * BLK:(v + 1) * BLK]
-            if s:
-                @pl.when(routes[s][1])
-                def _():
-                    part_copy(site, s, c).start()
+            for v in range(many):
+                parts[site, s, low + v] = product[:, v * BLK:(v + 1) * BLK]
+            if s == 3:
+                send(site, 2, c)
+            elif s == 2 and c in RIGHT_FIRST:
+                send(site, 1, c)
+            elif s == 1 and c not in RIGHT_FIRST:
+                send(site, 0, c)
 
     def out_copies(site, c):
-        span = pl.ds(c * CHUNK, CHUNK)
+        span = pl.ds(*SPANS[c])
         source, target = env.at[site + 1, span], out.at[0, core, 0, span]
         local = pltpu.make_async_copy(source, target, out_sem.at[c])
         remote = pltpu.make_async_remote_copy(
@@ -159,18 +188,17 @@
         return local, remote
 
     def combine(site, c):
-        for s, (step, sends, receives) in routes.items():
-            @pl.when(receives)
-            def _():
-                part_copy(site, s, c).wait_recv()
+        receive(site, 0, c)
+        receive(site, 1, c)
 
         size = pack[site, 4].astype(F32)[0:1]
         live = (lax.broadcasted_iota(jnp.int32, (BLK, BLK), 0).astype(F32) < size) & (
             lax.broadcasted_iota(jnp.int32, (BLK, BLK), 1).astype(F32) < size
         )
-        for v in range(c * CHUNK, (c + 1) * CHUNK):
+        low, many = SPANS[c]
+        for v in range(low, low + many):
             total = parts[site, 0, v].astype(F32) + got[site, 1, v].astype(F32)
-            total = total + got[site, 0, v].astype(F32) + got[site, 2, v].astype(F32)
+            total = total + got[site, 0, v].astype(F32)
             env[site + 1, v] = jnp.where(live, total, 0.0).astype(BF)
         local, remote = out_copies(site, c)
 
@@ -182,10 +210,11 @@
         def _():
             remote.start()
 
+    order = (0, 2, 1, 3)
     for site in range(2):
         await_site(site)
         prepare(site)
-        for c in range(CHUNKS):
+        for c in order:
             if site == 0:
                 env_copies[c].wait()
             else:
@@ -193,17 +222,19 @@
             project(site, c)
         for s in (3, 2, 1, 0):
             mix_and_send(site, s)
-    for c in range(CHUNKS):
+        for c in order:
+            pass_on(site, c)
+    for c in order:
         combine(1, c)
 
     for swap in swaps:
         swap.wait_send()
     for site in range(2):
-        for s, (step, sends, receives) in routes.items():
-            @pl.when(sends)
-            def _():
-                for c in range(CHUNKS):
-                    part_copy(site, s, c).wait_send()
+        for slot in range(3):
+            for c in range(CHUNKS):
+                @pl.when(route(slot, c)[2])
+                def _():
+                    part_copy(site, slot, c).wait_send()
     for site in range(2):
         for c in range(CHUNKS):
             local, remote = out_copies(site, c)
@@ -230,7 +261,7 @@
     return pl.pallas_call(
         kernel,
         out_shape=jax.ShapeDtypeStruct((1, 2, 1, W, BLK, BLK), BF),
-        in_specs=[anywhere] * 3,
+        in_specs=[pl.BlockSpec(memory_space=pltpu.HBM)] * 2 + [anywhere],
         out_specs=anywhere,
         scratch_shapes=[
             pltpu.VMEM((3, W, BLK, BLK), BF),
@@ -254,7 +285,7 @@
             pltpu.SemaphoreType.DMA((CHUNKS,)),
         ],
         compiler_params=pltpu.CompilerParams(
-            collective_id=0, has_side_effects=True, vmem_limit_bytes=48 * 1024 * 1024
+            collective_id=0, has_side_effects=True, vmem_limit_bytes=67043328
         ),
     )(env_first, states, pack)
 

time: 63.6 us -> 52.4 us (0.82)
  the two profiles are of different devices: /device:TPU:19 before, /device:TPU:5 now
where the time goes in v2:
time: 52.4 us; the launch traced here: 52.2 us
  Pallas kernels  47.8 us (91%)
  local copies, waits for them, and re-layouts  3.01 us (6%)
  other arithmetic  0.71 us (1%)
  between operations  0.69 us (1%)
    pallas_call x1, Pallas kernels, on_device(): pl.pallas_call(kernel, out_shape=jax.ShapeDtypeStruct((1, 2, 1, W, BLK, B...  47.8 us
    unnamed x6, local copies, waits for them, and re-layouts  3.01 us

profile of v2, /device:TPU:5, one launch (start us, length us, event | category | flops | bytes accessed | tf_op | source)
XLA Modules:
  0.0 52.2 jit_solution(992466610995778440)
XLA Ops:
  0.0 0.0 copy-start
  0.7 0.0 copy-start.1
  0.7 0.6 %copy-done.1 = s32[1,4,1]{1,2,0:T(1,128)S(1)} copy-done((s32[1,4,1]{1,2,0:T(1,128)S(1)}, s32[1,4,1]{1,2,0:T(1,128)}, u32[]{:S(2)}) %copy-start.1) | copy-done | bytes 40
  1.3 0.0 copy-done
  1.3 0.1 copy.6
  1.4 0.1 fusion.2
  1.5 0.6 %fusion.pack_in = bf16[5,16,128]{2,1,0:T(8,128)(2,1)} fusion(bf16[4,15,15]{2,1,0:T(8,128)(2,1)S(1)} %fusion.2, bf16[]{:T(256)} %bitcast.3), kind=kLoop, calls=%fused_computation.1 | loop fusion | flops 20480 | bytes 22282 | tf_op jit(solution)/shard_map/concatenate | solution.py:259
  2.2 47.8 %shard_map.55 = bf16[1,2,1,15,128,128]{5,4,3,2,1,0:T(8,128)(2,1)} custom-call(bf16[2,1,15,128,128]{4,3,2,1,0:T(8,128)(2,1)} %env_in.1, bf16[1,2,4,1,128,128]{5,4,3,2,1,0:T(8,128)(2,1)} %states_in.1, bf16[5,16,128]{2,1,0:T(8,128)(2,1)} %fusion.pack_in), custom_call_target="tpu_custom_call" | custom-call | tf_op jit(solution)/shard_map/pallas_call | solution.py:261
  50.0 2.2 %copy.9 = bf16[1,2,1,15,128,128]{5,4,3,2,1,0:T(8,128)(2,1)} copy(bf16[1,2,1,15,128,128]{5,4,3,2,1,0:T(8,128)(2,1)} %shard_map.55) | data formatting | bytes 1966080
  (1 shorter events, 0.0 us)
Async XLA Ops:
  0.0 1.3 %copy-start = (bf16[1,4,15,15]{3,1,2,0:T(4,128)(2,1)S(1)}, bf16[1,4,15,15]{3,1,2,0:T(4,128)(2,1)}, u32[]{:S(2)}) copy-start(bf16[1,4,15,15]{3,1,2,0:T(4,128)(2,1)} %param.7) | copy-start | bytes 5404
  0.7 0.7 %copy-start.1 = (s32[1,4,1]{1,2,0:T(1,128)S(1)}, s32[1,4,1]{1,2,0:T(1,128)}, u32[]{:S(2)}) copy-start(s32[1,4,1]{1,2,0:T(1,128)} %param.9) | copy-start | bytes 52

commit v3 on v1

v3 whole, which is shorter than its diff:
```python
import jax
import jax.numpy as jnp
from jax import lax
from jax.experimental import pallas as pl
from jax.experimental.pallas import tpu as pltpu
from jax.sharding import PartitionSpec as P

QD = 4
W = 15
BLK = 128
SUB = 16
SPANS = ((0, 4), (4, 4), (8, 4), (12, 3))
CHUNKS = len(SPANS)
MESH = pl.DeviceIdType.MESH
BF = jnp.bfloat16
F32 = jnp.float32


def kernel(
    env_in, states_in, pack_in, out,
    env, near_env, blocks, near_blocks, pack, near_pack, joined, turned, kron, proj, mixed, parts, merged, got,
    env_sem, own_sem, swap_send, swap_recv, near_send, near_recv, env_send, env_recv, got_send, got_recv,
    out_sem, out_send, out_recv,
):
    sectors = lax.axis_size("sector")
    core, k = lax.axis_index("chain"), lax.axis_index("sector")
    other = 1 - core
    down = lax.rem(k, QD)
    right = (jnp.int32(1), down < QD - 1, down > 0)
    up = (jnp.int32(QD), k < sectors - QD, k >= QD)
    first = tuple(jnp.where(core == 0, r, u) for r, u in zip(right, up))
    second = tuple(jnp.where(core == 0, u, r) for r, u in zip(right, up))
    step, goes, comes = first
    step_after, goes_after, comes_after = second
    state_first = jnp.where(core == 0, 2, 1)
    state_after = 3 - state_first

    own_blocks = pltpu.make_async_copy(states_in.at[0, core, :, 0], blocks.at[core], own_sem.at[0])
    own_pack = pltpu.make_async_copy(pack_in, pack.at[core], own_sem.at[1])
    own_env = [
        pltpu.make_async_copy(env_in.at[core, 0, pl.ds(*SPANS[c])], env.at[0, pl.ds(*SPANS[c])], env_sem.at[c])
        for c in range(CHUNKS)
    ]
    own_blocks.start()
    own_pack.start()
    for copy in own_env:
        copy.start()

    barrier = pltpu.get_barrier_semaphore()

    def greet(condition, device):
        @pl.when(condition)
        def _():
            pl.semaphore_signal(barrier, inc=1, device_id=device, device_id_type=MESH)

    pl.semaphore_signal(barrier, inc=1, device_id=(other, k), device_id_type=MESH)
    greet(goes, (core, k + step))
    greet(comes, (core, k - step))
    greet(goes_after, (core, k + step_after))
    greet(comes_after, (core, k - step_after))
    greet(goes_after, (other, k + step_after))
    greet(comes, (other, k - step))
    pl.semaphore_wait(
        barrier,
        1 + 2 * goes_after.astype(jnp.int32) + 2 * comes.astype(jnp.int32)
        + goes.astype(jnp.int32) + comes_after.astype(jnp.int32),
    )

    def remote(source, target, send_sem, recv_sem, device):
        return pltpu.make_async_remote_copy(
            src_ref=source, dst_ref=target, send_sem=send_sem, recv_sem=recv_sem,
            device_id=device, device_id_type=MESH,
        )

    def when_do(condition, copies, action):
        @pl.when(condition)
        def _():
            for copy in copies:
                getattr(copy, action)()

    def near_copies(site, target, state, device, way):
        return [
            remote(source, sink, near_send.at[way, i], near_recv.at[site, i], device)
            for i, (source, sink) in enumerate([
                (pack_in, near_pack.at[site]),
                (states_in.at[0, target, 3, 0], near_blocks.at[site, 1]),
                (states_in.at[0, target, state, 0], near_blocks.at[site, 0]),
            ])
        ]

    def env_copy(site, c):
        span = pl.ds(*SPANS[c])
        source = env_in.at[core, 0, span] if site == 0 else env.at[1, span]
        return remote(
            source, near_env.at[site, span], env_send.at[site, c], env_recv.at[site, c], (core, k + step)
        )

    def got_copy(site, c):
        span = pl.ds(*SPANS[c])
        return remote(
            merged.at[site, span], got.at[site, span], got_send.at[site, c], got_recv.at[site, c],
            (core, k + step_after),
        )

    swaps = [
        remote(source, target, swap_send.at[i], swap_recv.at[i], (other, k))
        for i, (source, target) in enumerate(
            [(pack_in, pack.at[core]), (states_in.at[0, other, :, 0], blocks.at[core])]
        )
    ]
    near_same = near_copies(core, core, state_first, (core, k + step), 0)
    near_other = near_copies(core, other, state_after, (other, k + step_after), 1)
    for swap in swaps:
        swap.start()
    when_do(goes, near_same, "start")
    when_do(goes_after, near_other, "start")
    when_do(goes, [env_copy(0, c) for c in range(CHUNKS)], "start")

    proj[:, W] = jnp.zeros((2, BLK, 2 * BLK), BF)

    @pl.when(jnp.logical_not(comes))
    def _():
        near_blocks[...] = jnp.zeros_like(near_blocks)
        near_pack[...] = jnp.zeros_like(near_pack)
        near_env[...] = jnp.zeros_like(near_env)

    @pl.when(jnp.logical_not(comes_after))
    def _():
        got[...] = jnp.zeros_like(got)

    def prepare(q, coupling, block):
        spread = (lax.broadcasted_iota(jnp.int32, (W * SUB, SUB), 0) >> 4) == lax.broadcasted_iota(
            jnp.int32, (W * SUB, SUB), 1
        )
        spread = jnp.where(spread, 1.0, 0.0).astype(BF)
        widen = lax.broadcasted_iota(jnp.int32, (BLK, 256), 0) == (
            lax.broadcasted_iota(jnp.int32, (BLK, 256), 1) >> 4
        )
        widen = jnp.where(widen, 1.0, 0.0).astype(BF)
        same = (lax.broadcasted_iota(jnp.int32, (W * SUB, 256), 0) & 15) == (
            lax.broadcasted_iota(jnp.int32, (W * SUB, 256), 1) & 15
        )
        tall = jnp.dot(spread, coupling, preferred_element_type=F32).astype(BF)
        wide = jnp.dot(tall, widen, preferred_element_type=F32)
        kron[q] = jnp.where(same, wide, 0.0).astype(BF)
        joined[q // 2, :, (q % 2) * BLK:(q % 2 + 1) * BLK] = block
        turned[q] = block.astype(F32).T.astype(BF)

    def prepare_own(site):
        @pl.when(core == site)
        def _():
            own_blocks.wait()
            own_pack.wait()

        when_do(core != site, swaps, "wait_recv")
        prepare(0, pack[site, 0], blocks[site, 0])
        prepare(1, pack[site, state_after], blocks[site, state_after])

    def prepare_near(site):
        when_do(comes, near_copies(site, core, state_first, (core, k + step), 0), "wait_recv")
        prepare(2, near_pack[site, state_first], near_blocks[site, 0])
        prepare(3, near_pack[site, 3], near_blocks[site, 1])

    def project(half, source, c):
        low, many = SPANS[c]
        rows = source[low:low + many].reshape(many * BLK, BLK)
        product = jnp.dot(rows, joined[half], preferred_element_type=F32).astype(BF)
        proj[half, low:low + many] = product.reshape(many, BLK, 2 * BLK)

    def mix(site, q):
        half, lanes = q // 2, slice((q % 2) * BLK, (q % 2 + 1) * BLK)
        for i in range(BLK // (2 * SUB)):
            low, mid, high = 2 * i * SUB, (2 * i + 1) * SUB, (2 * i + 2) * SUB
            pair = jnp.concatenate(
                [proj[half, :, low:mid, lanes].reshape(256, BLK), proj[half, :, mid:high, lanes].reshape(256, BLK)],
                axis=1,
            )
            product = jnp.dot(kron[q], pair, preferred_element_type=F32).astype(BF)
            for v in range(W):
                mixed[low:mid, v * BLK:(v + 1) * BLK] = product[v * SUB:(v + 1) * SUB, :BLK]
                mixed[mid:high, v * BLK:(v + 1) * BLK] = product[v * SUB:(v + 1) * SUB, BLK:]
        for c, (low, many) in enumerate(SPANS):
            product = jnp.dot(
                turned[q], mixed[:, low * BLK:(low + many) * BLK], preferred_element_type=F32
            )
            for v in range(many):
                part = product[:, v * BLK:(v + 1) * BLK]
                if q == 3:
                    merged[site, low + v] = (part + parts[1, low + v].astype(F32)).astype(BF)
                else:
                    parts[q, low + v] = part.astype(BF)
            if q == 3:
                when_do(goes_after, [got_copy(site, c)], "start")

    def out_copies(site, c):
        span = pl.ds(*SPANS[c])
        source, target = env.at[site + 1, span], out.at[0, core, 0, span]
        local = pltpu.make_async_copy(source, target, out_sem.at[c])
        return local, remote(source, target, out_send.at[c], out_recv.at[c], (other, k))

    def combine(site, c):
        when_do(comes_after, [got_copy(site, c)], "wait_recv")
        size = pack[site, 4].astype(F32)[0:1]
        live = (lax.broadcasted_iota(jnp.int32, (BLK, BLK), 0).astype(F32) < size) & (
            lax.broadcasted_iota(jnp.int32, (BLK, BLK), 1).astype(F32) < size
        )
        low, many = SPANS[c]
        for v in range(low, low + many):
            total = parts[0, v].astype(F32) + parts[2, v].astype(F32) + got[site, v].astype(F32)
            env[site + 1, v] = jnp.where(live, total, 0.0).astype(BF)
        if site == 0:
            when_do(goes, [env_copy(1, c)], "start")
        local, across = out_copies(site, c)
        when_do(core == site, [local], "start")
        when_do(core != site, [across], "start")

    for site in range(2):
        prepare_own(site)
        if site == 1:
            prepare_near(site)
        for c in range(CHUNKS):
            if site == 0:
                own_env[c].wait()
            else:
                combine(0, c)
            project(0, env.at[site], c)
        mix(site, 1)
        mix(site, 0)
        if site == 0:
            prepare_near(site)
        for c in range(CHUNKS):
            when_do(comes, [env_copy(site, c)], "wait_recv")
            project(1, near_env.at[site], c)
        mix(site, 3)
        mix(site, 2)
    for c in range(CHUNKS):
        combine(1, c)

    for swap in swaps:
        swap.wait_send()
    when_do(goes, near_same, "wait_send")
    when_do(goes_after, near_other, "wait_send")
    for site in range(2):
        when_do(goes, [env_copy(site, c) for c in range(CHUNKS)], "wait_send")
        when_do(goes_after, [got_copy(site, c) for c in range(CHUNKS)], "wait_send")
    for site in range(2):
        for c in range(CHUNKS):
            local, across = out_copies(site, c)
            @pl.when(core == site)
            def _():
                local.wait()
                across.wait_recv()

            when_do(core != site, [across], "wait_send")


def on_device(env_first, states, mpo, block_rows, present):
    down_charge = lax.axis_index("sector") % QD
    inside = jnp.where(jnp.arange(4) >= 2, (down_charge < QD - 1).astype(F32), 1.0)
    keep = present[0, :, 0].astype(F32) * inside
    coupling = jnp.swapaxes(mpo[0], 1, 2).astype(F32) * keep[:, None, None]
    coupling = jnp.pad(coupling, ((0, 0), (0, SUB - W), (0, BLK - W)))
    size = jnp.broadcast_to(block_rows[0, 0].astype(F32), (1, SUB, BLK))
    pack = jnp.concatenate([coupling, size], axis=0).astype(BF)
    anywhere = pl.BlockSpec(memory_space=pl.ANY)
    return pl.pallas_call(
        kernel,
        out_shape=jax.ShapeDtypeStruct((1, 2, 1, W, BLK, BLK), BF),
        in_specs=[pl.BlockSpec(memory_space=pltpu.HBM)] * 2 + [anywhere],
        out_specs=anywhere,
        scratch_shapes=[
            pltpu.VMEM((3, W, BLK, BLK), BF),
            pltpu.VMEM((2, W, BLK, BLK), BF),
            pltpu.VMEM((2, 4, BLK, BLK), BF),
            pltpu.VMEM((2, 2, BLK, BLK), BF),
            pltpu.VMEM((2, 5, SUB, BLK), BF),
            pltpu.VMEM((2, 5, SUB, BLK), BF),
            pltpu.VMEM((2, BLK, 2 * BLK), BF),
            pltpu.VMEM((4, BLK, BLK), BF),
            pltpu.VMEM((4, W * SUB, 256), BF),
            pltpu.VMEM((2, W + 1, BLK, 2 * BLK), BF),
            pltpu.VMEM((BLK, W * BLK), BF),
            pltpu.VMEM((3, W, BLK, BLK), BF),
            pltpu.VMEM((2, W, BLK, BLK), BF),
            pltpu.VMEM((2, W, BLK, BLK), BF),
            pltpu.SemaphoreType.DMA((CHUNKS,)),
            pltpu.SemaphoreType.DMA((2,)),
            pltpu.SemaphoreType.DMA((2,)),
            pltpu.SemaphoreType.DMA((2,)),
            pltpu.SemaphoreType.DMA((2, 3)),
            pltpu.SemaphoreType.DMA((2, 3)),
            pltpu.SemaphoreType.DMA((2, CHUNKS)),
            pltpu.SemaphoreType.DMA((2, CHUNKS)),
            pltpu.SemaphoreType.DMA((2, CHUNKS)),
            pltpu.SemaphoreType.DMA((2, CHUNKS)),
            pltpu.SemaphoreType.DMA((CHUNKS,)),
            pltpu.SemaphoreType.DMA((CHUNKS,)),
            pltpu.SemaphoreType.DMA((CHUNKS,)),
        ],
        compiler_params=pltpu.CompilerParams(
            collective_id=0, has_side_effects=True, vmem_limit_bytes=67043328
        ),
    )(env_first, states, pack)


def solution(mesh):
    placed = (
        P(None, "sector", None, None, None),
        P("chain", None, None, "sector", None, None),
        P("chain", None, None, None),
        P("chain", "sector"),
        P("chain", None, "sector"),
    )
    return jax.shard_map(
        on_device,
        mesh=mesh,
        in_specs=placed,
        out_specs=P("chain", None, "sector", None, None, None),
        check_vma=False,
    )
```

time: 63.6 us -> 49.5 us (0.78)
  the two profiles are of different devices: /device:TPU:19 before, /device:TPU:23 now
where the time goes in v3:
time: 49.5 us; the launch traced here: 49.2 us
  Pallas kernels  44.8 us (91%)
  local copies, waits for them, and re-layouts  3.01 us (6%)
  other arithmetic  0.71 us (1%)
  between operations  0.69 us (1%)
    pallas_call x1, Pallas kernels, on_device(): pl.pallas_call(kernel, out_shape=jax.ShapeDtypeStruct((1, 2, 1, W, BLK, B...  44.8 us
    unnamed x6, local copies, waits for them, and re-layouts  3.01 us

profile of v3, /device:TPU:23, one launch (start us, length us, event | category | flops | bytes accessed | tf_op | source)
XLA Modules:
  0.0 49.2 jit_solution(3463624141487550235)
XLA Ops:
  0.0 0.0 copy-start
  0.7 0.0 copy-start.1
  0.7 0.6 %copy-done.1 = s32[1,4,1]{1,2,0:T(1,128)S(1)} copy-done((s32[1,4,1]{1,2,0:T(1,128)S(1)}, s32[1,4,1]{1,2,0:T(1,128)}, u32[]{:S(2)}) %copy-start.1) | copy-done | bytes 40
  1.3 0.0 copy-done
  1.3 0.1 copy.6
  1.4 0.1 fusion.2
  1.5 0.6 %fusion.pack_in = bf16[5,16,128]{2,1,0:T(8,128)(2,1)} fusion(bf16[4,15,15]{2,1,0:T(8,128)(2,1)S(1)} %fusion.2, bf16[]{:T(256)} %bitcast.3), kind=kLoop, calls=%fused_computation.1 | loop fusion | flops 20480 | bytes 22282 | tf_op jit(solution)/shard_map/concatenate | solution.py:264
  2.2 44.8 %shard_map.55 = bf16[1,2,1,15,128,128]{5,4,3,2,1,0:T(8,128)(2,1)} custom-call(bf16[2,1,15,128,128]{4,3,2,1,0:T(8,128)(2,1)} %env_in.1, bf16[1,2,4,1,128,128]{5,4,3,2,1,0:T(8,128)(2,1)} %states_in.1, bf16[5,16,128]{2,1,0:T(8,128)(2,1)} %fusion.pack_in), custom_call_target="tpu_custom_call" | custom-call | tf_op jit(solution)/shard_map/pallas_call | solution.py:266
  47.0 2.2 %copy.9 = bf16[1,2,1,15,128,128]{5,4,3,2,1,0:T(8,128)(2,1)} copy(bf16[1,2,1,15,128,128]{5,4,3,2,1,0:T(8,128)(2,1)} %shard_map.55) | data formatting | bytes 1966080
  (1 shorter events, 0.0 us)
Async XLA Ops:
  0.0 1.3 %copy-start = (bf16[1,4,15,15]{3,1,2,0:T(4,128)(2,1)S(1)}, bf16[1,4,15,15]{3,1,2,0:T(4,128)(2,1)}, u32[]{:S(2)}) copy-start(bf16[1,4,15,15]{3,1,2,0:T(4,128)(2,1)} %param.7) | copy-start | bytes 5404
  0.7 0.7 %copy-start.1 = (s32[1,4,1]{1,2,0:T(1,128)S(1)}, s32[1,4,1]{1,2,0:T(1,128)}, u32[]{:S(2)}) copy-start(s32[1,4,1]{1,2,0:T(1,128)} %param.9) | copy-start | bytes 52

commit v4 on v3

--- a/solution.py
+++ b/solution.py
@@ -112,9 +112,11 @@
     near_other = near_copies(core, other, state_after, (other, k + step_after), 1)
     for swap in swaps:
         swap.start()
-    when_do(goes, near_same, "start")
-    when_do(goes_after, near_other, "start")
+    when_do(goes & (core == 0), near_same, "start")
+    when_do(goes_after & (core == 0), near_other, "start")
     when_do(goes, [env_copy(0, c) for c in range(CHUNKS)], "start")
+    when_do(goes & (core == 1), near_same, "start")
+    when_do(goes_after & (core == 1), near_other, "start")
 
     proj[:, W] = jnp.zeros((2, BLK, 2 * BLK), BF)
 
@@ -298,9 +300,13 @@
             pltpu.SemaphoreType.DMA((CHUNKS,)),
         ],
         compiler_params=pltpu.CompilerParams(
-            collective_id=0, has_side_effects=True, vmem_limit_bytes=67043328
+            collective_id=0, has_side_effects=True, vmem_limit_bytes=48 * 1024 * 1024
         ),
-    )(env_first, states, pack)
+    )(
+        pltpu.with_memory_space_constraint(env_first, pltpu.HBM),
+        pltpu.with_memory_space_constraint(states, pltpu.HBM),
+        pack,
+    )
 
 
 def solution(mesh):

time: 49.5 us -> 47 us (0.949)
  local copies, waits for them, and re-layouts: 3.01 us -> 1.71 us
  other arithmetic: 0.71 us -> 0.1 us
  Pallas kernels: 44.8 us -> 44.3 us
    unnamed x6, local copies, waits for them, and re-layouts: 3.01 us -> 1.71 us
    concatenate x1, other arithmetic: 0.63 us -> 0.02 us  [on_device(): pack = jnp.concatenate([coupling, size], axis=0).astype(BF)]
where the time goes in v4:
time: 47 us; the launch traced here: 46.8 us
  Pallas kernels  44.3 us (94%)
  local copies, waits for them, and re-layouts  1.71 us (4%)
  between operations  0.69 us (1%)
    pallas_call x1, Pallas kernels, on_device(): pl.pallas_call(kernel, out_shape=jax.ShapeDtypeStruct((1, 2, 1, W, BLK, B...  44.3 us
    unnamed x6, local copies, waits for them, and re-layouts  1.71 us

profile of v4, /device:TPU:23, one launch (start us, length us, event | category | flops | bytes accessed | tf_op | source)
XLA Modules:
  0.0 46.8 jit_solution(13431224628483847402)
XLA Ops:
  0.0 0.0 copy-start
  0.7 0.0 copy-start.1
  0.7 0.6 %copy-done.1 = s32[1,4,1]{1,2,0:T(1,128)S(1)} copy-done((s32[1,4,1]{1,2,0:T(1,128)S(1)}, s32[1,4,1]{1,2,0:T(1,128)}, u32[]{:S(2)}) %copy-start.1) | copy-done | bytes 40
  1.3 0.0 copy-done
  1.3 0.1 copy.6
  1.4 0.1 fusion.2
  1.5 44.3 %shard_map.55 = bf16[1,2,1,15,128,128]{5,4,3,2,1,0:T(8,128)(2,1)S(1)} custom-call(bf16[2,1,15,128,128]{4,3,2,1,0:T(8,128)(2,1)} %env_in.1, bf16[1,2,4,1,128,128]{5,4,3,2,1,0:T(8,128)(2,1)} %states_in.1, bf16[5,16,128]{2,1,0:T(8,128)(2,1)S(1)} %fusion.pack_in), custom_call_target="tpu_custom_call" | custom-call | tf_op jit(solution)/shard_map/pallas_call | solution.py:268
  45.9 0.9 %copy.9 = bf16[1,2,1,15,128,128]{5,4,3,2,1,0:T(8,128)(2,1)} copy(bf16[1,2,1,15,128,128]{5,4,3,2,1,0:T(8,128)(2,1)S(1)} %shard_map.55) | data formatting | bytes 1966080
  (2 shorter events, 0.0 us)
Async XLA Ops:
  0.0 1.3 %copy-start = (bf16[1,4,15,15]{3,1,2,0:T(4,128)(2,1)S(1)}, bf16[1,4,15,15]{3,1,2,0:T(4,128)(2,1)}, u32[]{:S(2)}) copy-start(bf16[1,4,15,15]{3,1,2,0:T(4,128)(2,1)} %param.7) | copy-start | bytes 5404
  0.7 0.7 %copy-start.1 = (s32[1,4,1]{1,2,0:T(1,128)S(1)}, s32[1,4,1]{1,2,0:T(1,128)}, u32[]{:S(2)}) copy-start(s32[1,4,1]{1,2,0:T(1,128)} %param.9) | copy-start | bytes 52

commit v5 on v4

--- a/solution.py
+++ b/solution.py
@@ -9,7 +9,7 @@
 W = 15
 BLK = 128
 SUB = 16
-SPANS = ((0, 4), (4, 4), (8, 4), (12, 3))
+SPANS = ((0, 4), (4, 4), (8, 4), (12, 2), (14, 1))
 CHUNKS = len(SPANS)
 MESH = pl.DeviceIdType.MESH
 BF = jnp.bfloat16

time: 47 us -> 46.4 us (0.987)
  Pallas kernels: 44.3 us -> 43.7 us
    pallas_call x1, Pallas kernels: 44.3 us -> 43.7 us  [on_device(): pl.pallas_call(kernel, out_shape=jax.ShapeDtypeStruct((1, 2, 1, W, BLK, B...]
where the time goes in v5:
time: 46.4 us; the launch traced here: 46.2 us
  Pallas kernels  43.7 us (94%)
  local copies, waits for them, and re-layouts  1.71 us (4%)
  between operations  0.69 us (1%)
    pallas_call x1, Pallas kernels, on_device(): pl.pallas_call(kernel, out_shape=jax.ShapeDtypeStruct((1, 2, 1, W, BLK, B...  43.7 us
    unnamed x6, local copies, waits for them, and re-layouts  1.71 us

profile of v5, /device:TPU:23, one launch (start us, length us, event | category | flops | bytes accessed | tf_op | source)
XLA Modules:
  0.0 46.2 jit_solution(7304177816757736754)
XLA Ops:
  0.0 0.0 copy-start
  0.7 0.0 copy-start.1
  0.7 0.6 %copy-done.1 = s32[1,4,1]{1,2,0:T(1,128)S(1)} copy-done((s32[1,4,1]{1,2,0:T(1,128)S(1)}, s32[1,4,1]{1,2,0:T(1,128)}, u32[]{:S(2)}) %copy-start.1) | copy-done | bytes 40
  1.3 0.0 copy-done
  1.3 0.1 copy.6
  1.4 0.1 fusion.2
  1.5 43.7 %shard_map.55 = bf16[1,2,1,15,128,128]{5,4,3,2,1,0:T(8,128)(2,1)S(1)} custom-call(bf16[2,1,15,128,128]{4,3,2,1,0:T(8,128)(2,1)} %env_in.1, bf16[1,2,4,1,128,128]{5,4,3,2,1,0:T(8,128)(2,1)} %states_in.1, bf16[5,16,128]{2,1,0:T(8,128)(2,1)S(1)} %fusion.pack_in), custom_call_target="tpu_custom_call" | custom-call | tf_op jit(solution)/shard_map/pallas_call | solution.py:268
  45.3 0.9 %copy.9 = bf16[1,2,1,15,128,128]{5,4,3,2,1,0:T(8,128)(2,1)} copy(bf16[1,2,1,15,128,128]{5,4,3,2,1,0:T(8,128)(2,1)S(1)} %shard_map.55) | data formatting | bytes 1966080
  (2 shorter events, 0.0 us)
Async XLA Ops:
  0.0 1.3 %copy-start = (bf16[1,4,15,15]{3,1,2,0:T(4,128)(2,1)S(1)}, bf16[1,4,15,15]{3,1,2,0:T(4,128)(2,1)}, u32[]{:S(2)}) copy-start(bf16[1,4,15,15]{3,1,2,0:T(4,128)(2,1)} %param.7) | copy-start | bytes 5404
  0.7 0.7 %copy-start.1 = (s32[1,4,1]{1,2,0:T(1,128)S(1)}, s32[1,4,1]{1,2,0:T(1,128)}, u32[]{:S(2)}) copy-start(s32[1,4,1]{1,2,0:T(1,128)} %param.9) | copy-start | bytes 52

commit v6 on v5

--- a/solution.py
+++ b/solution.py
@@ -227,7 +227,6 @@
                 combine(0, c)
             project(0, env.at[site], c)
         mix(site, 1)
-        mix(site, 0)
         if site == 0:
             prepare_near(site)
         for c in range(CHUNKS):
@@ -235,6 +234,7 @@
             project(1, near_env.at[site], c)
         mix(site, 3)
         mix(site, 2)
+        mix(site, 0)
     for c in range(CHUNKS):
         combine(1, c)
 

time: 46.4 us -> 47.1 us (1.015)
  Pallas kernels: 43.7 us -> 44.4 us
    pallas_call x1, Pallas kernels: 43.7 us -> 44.4 us  [on_device(): pl.pallas_call(kernel, out_shape=jax.ShapeDtypeStruct((1, 2, 1, W, BLK, B...]
where the time goes in v6:
time: 47.1 us; the launch traced here: 46.9 us
  Pallas kernels  44.4 us (94%)
  local copies, waits for them, and re-layouts  1.71 us (4%)
  between operations  0.69 us (1%)
    pallas_call x1, Pallas kernels, on_device(): pl.pallas_call(kernel, out_shape=jax.ShapeDtypeStruct((1, 2, 1, W, BLK, B...  44.4 us
    unnamed x6, local copies, waits for them, and re-layouts  1.71 us

profile of v6, /device:TPU:23, one launch (start us, length us, event | category | flops | bytes accessed | tf_op | source)
XLA Modules:
  0.0 46.9 jit_solution(2850327394408411905)
XLA Ops:
  0.0 0.0 copy-start
  0.7 0.0 copy-start.1
  0.7 0.6 %copy-done.1 = s32[1,4,1]{1,2,0:T(1,128)S(1)} copy-done((s32[1,4,1]{1,2,0:T(1,128)S(1)}, s32[1,4,1]{1,2,0:T(1,128)}, u32[]{:S(2)}) %copy-start.1) | copy-done | bytes 40
  1.3 0.0 copy-done
  1.3 0.1 copy.6
  1.4 0.1 fusion.2
  1.5 44.4 %shard_map.55 = bf16[1,2,1,15,128,128]{5,4,3,2,1,0:T(8,128)(2,1)S(1)} custom-call(bf16[2,1,15,128,128]{4,3,2,1,0:T(8,128)(2,1)} %env_in.1, bf16[1,2,4,1,128,128]{5,4,3,2,1,0:T(8,128)(2,1)} %states_in.1, bf16[5,16,128]{2,1,0:T(8,128)(2,1)S(1)} %fusion.pack_in), custom_call_target="tpu_custom_call" | custom-call | tf_op jit(solution)/shard_map/pallas_call | solution.py:268
  46.0 0.9 %copy.9 = bf16[1,2,1,15,128,128]{5,4,3,2,1,0:T(8,128)(2,1)} copy(bf16[1,2,1,15,128,128]{5,4,3,2,1,0:T(8,128)(2,1)S(1)} %shard_map.55) | data formatting | bytes 1966080
  (2 shorter events, 0.0 us)
Async XLA Ops:
  0.0 1.3 %copy-start = (bf16[1,4,15,15]{3,1,2,0:T(4,128)(2,1)S(1)}, bf16[1,4,15,15]{3,1,2,0:T(4,128)(2,1)}, u32[]{:S(2)}) copy-start(bf16[1,4,15,15]{3,1,2,0:T(4,128)(2,1)} %param.7) | copy-start | bytes 5404
  0.7 0.7 %copy-start.1 = (s32[1,4,1]{1,2,0:T(1,128)S(1)}, s32[1,4,1]{1,2,0:T(1,128)}, u32[]{:S(2)}) copy-start(s32[1,4,1]{1,2,0:T(1,128)} %param.9) | copy-start | bytes 52
